TPU v7x, 512 devices: a whole 4x8x8 slice. The times are simulated.
512 devices in a mesh: group: 16 (over y, core), inner: 32 (over x, z).
Axes of the slice: x: 4, y: 8, z: 8, core: 2. Of those that a mesh axis runs over, the one named last changes fastest.
Arguments:
- pair_rows: bfloat16 [8192, 2048], P(('group', 'inner')), may hold values from -6 to 6
- group_ids: int32 [8192, 1], P(('group', 'inner')), may hold values from 0 to 15; in each aligned block of 16 rows (0 to 15, 16 to 31, ...) at most 2 rows name the same one
- local_ids: int32 [8192, 1], P(('group', 'inner')), may hold values from 0 to 1
- route_weight: float32 [8192], P(('group', 'inner')), may hold values from 0.3 to 1
- w_up: bfloat16 [32, 2048, 8192], P('group', None, 'inner'), may hold values from -0.125 to 0.125
- w_down: bfloat16 [32, 8192, 2048], P('group', 'inner'), may hold values from -0.0625 to 0.0625
Outputs:
- mixed: bfloat16 [8192, 2048], P(('group', 'inner'))
Inputs may be any that keep to these rules, and one draw needn't show every extreme that they name: `group_ids`: among the rows of one device no value is named more than 2 times, a bound that some block reaches.
All inputs are finite; a program needn't handle non-finite values.
Results may differ from a plain program's by a relative error of at most 0.02.
Values may be sent and summed in bfloat16 or wider, within the bound.
A program may use at most 64 MiB of HBM per device.

v0:
```python
import jax
import jax.numpy as jnp
from jax import lax
from jax.sharding import PartitionSpec as P


def body(pair_rows, group_ids, local_ids, route_weight, w_up, w_down):
    groups = lax.axis_size("group")
    inner_size = lax.axis_size("inner")
    count_rows = pair_rows.shape[0]
    model_width = pair_rows.shape[1]
    local_count = w_up.shape[0]
    capacity = 2 * count_rows // groups
    group_of = group_ids[:, 0]
    onehot = (group_of[:, None] == jnp.arange(groups, dtype=jnp.int32)[None, :]).astype(jnp.int32)
    rank_in = jnp.sum((jnp.cumsum(onehot, 0) - onehot) * onehot, 1)
    target = group_of * capacity + rank_in
    placing = (jnp.arange(groups * capacity, dtype=jnp.int32)[:, None] == target[None, :]).astype(
        jnp.bfloat16
    )
    outgoing = jnp.dot(placing, pair_rows, preferred_element_type=jnp.float32).astype(jnp.bfloat16)
    outgoing = outgoing.reshape(1, groups, capacity, model_width)
    tag_rows = (local_ids[:, 0] + 1).astype(jnp.bfloat16)
    tags = jnp.dot(placing, tag_rows, preferred_element_type=jnp.float32).astype(jnp.bfloat16)
    tags = tags.reshape(1, groups, capacity)
    arrived, arrived_tags = (
        lax.all_to_all(outgoing, "group", split_axis=1, concat_axis=1, tiled=True),
        lax.all_to_all(tags, "group", split_axis=1, concat_axis=1, tiled=True),
    )
    gathered, gathered_tags = (
        lax.all_gather(arrived, "inner", axis=0, tiled=True),
        lax.all_gather(arrived_tags, "inner", axis=0, tiled=True),
    )
    slots = gathered.reshape(inner_size * groups * capacity, model_width)
    slot_tags = gathered_tags.reshape(inner_size * groups * capacity).astype(jnp.float32)
    expert_index = jnp.arange(local_count, dtype=jnp.float32) + 1.0
    own_rows = groups * capacity
    selector = (slot_tags[:, None] == expert_index[None, :]).astype(jnp.float32)
    up_val = jnp.einsum("rd,edf->ref", slots, w_up, preferred_element_type=jnp.float32)
    hidden = (jax.nn.silu(up_val) * selector[:, :, None]).astype(jnp.bfloat16)
    every_term = jnp.einsum("ref,efd->rd", hidden, w_down, preferred_element_type=jnp.float32)
    totals = lax.psum(every_term.astype(jnp.bfloat16), "inner").astype(jnp.float32)
    summed = lax.dynamic_slice_in_dim(totals, lax.axis_index("inner") * own_rows, own_rows, 0)
    send_back = summed.astype(jnp.bfloat16).reshape(groups, capacity, model_width)
    returned = lax.all_to_all(send_back, "group", split_axis=0, concat_axis=0, tiled=True)
    combined = jnp.dot(
        placing.T,
        returned.reshape(groups * capacity, model_width),
        preferred_element_type=jnp.float32,
    )
    return (combined * route_weight[:, None]).astype(jnp.bfloat16)


def solution(mesh):
    placed = (
        P(("group", "inner"), None),
        P(("group", "inner"), None),
        P(("group", "inner"), None),
        P(("group", "inner")),
        P("group", None, "inner"),
        P("group", "inner", None),
    )
    return jax.shard_map(
        body, mesh=mesh, in_specs=placed, out_specs=P(("group", "inner"), None), check_vma=False
    )
```

profile of v0, /device:TPU:1, one launch (start us, length us, event | category | flops | bytes accessed | tf_op | source)
XLA Modules:
  0.0 338.9 jit_solution(1572055282033931939)
XLA Ops:
  6.5 0.9 fusion.5
  7.5 0.8 select_reduce_fusion
  8.3 0.7 multiply_add_fusion
  9.0 1.0 convolution_convert_fusion
  10.0 0.1 reshape.67
  10.1 18.5 %all_to_all.15 = bf16[1,16,2,2048]{3,2,0,1:T(2,128)(2,1)S(1)} all-to-all(bf16[1,16,2,2048]{3,2,0,1:T(2,128)(2,1)S(1)} %bitcast.15), channel_id=1, replica_groups=mesh['group'=16,'inner'=32] {'group'}, dimensions={1} | all-to-all | bytes 262144 | tf_op jit(solution)/shard_map/all_to_all | solution.py:27
  28.6 0.7 copy.14
  29.3 0.8 fusion.1
  30.1 0.7 reshape.78
  30.8 3.4 all-to-all-start.1
  34.2 6.5 %all-to-all-done.1 = bf16[1,16,2]{2,0,1:T(2,128)(2,1)S(1)} async-done(((bf16[1,16,2]{2,0,1:T(2,128)(2,1)}), bf16[1,16,2]{2,0,1:T(2,128)(2,1)S(1)}, u32[]{:S(2)}, u32[]{:S(2)}) %all-to-all-start.1) | async-done | bytes 96 | tf_op jit(solution)/shard_map/all_to_all | solution.py:28
  40.7 0.1 copy.17
  40.8 37.2 %all_gather.7 = bf16[32,16,2]{1,2,0:T(2,128)(2,1)S(1)} all-gather(bf16[1,16,2]{1,2,0:T(2,128)(2,1)S(1)} %copy.17), channel_id=1, replica_groups=mesh['group'=16,'inner'=32] {'inner'}, dimensions={0}, use_global_device_ids=true | all-gather | bytes 2112 | tf_op jit(solution)/shard_map/all_gather | solution.py:32
  78.1 0.2 copy.19
  78.3 0.2 reshape.72
  78.5 34.5 %all-gather.2.cloned.1.call-done = bf16[32,16,2,2048]{3,1,2,0:T(8,128)(2,1)} async-done(((bf16[1,16,2,2048]{3,1,2,0:T(8,128)(2,1)}), bf16[32,16,2,2048]{3,1,2,0:T(8,128)(2,1)}) %all-gather.2.cloned.1.call-update) | async-done | bytes 4194320 | tf_op jit(solution)/shard_map/all_gather | solution.py:31
  113.1 8.5 %copy.15 = bf16[32,16,2,2048]{3,2,1,0:T(2,128)(2,1)} copy(bf16[32,16,2,2048]{3,1,2,0:T(8,128)(2,1)} %all-gather.2.cloned.1.call-done) | data formatting | bytes 8388608 | tf_op jit(solution)/shard_map/all_gather | solution.py:31
  121.6 7.2 %reshape.73 = bf16[1024,2048,1]{1,0,2:T(8,128)(2,1)} reshape(bf16[32,16,2,2048]{3,2,1,0:T(2,128)(2,1)} %copy.15) | data formatting | bytes 8388608 | tf_op jit(solution)/shard_map/reshape | solution.py:34
  128.8 9.5 %bitcast_convert_fusion = bf16[1024,2048]{1,0:T(8,128)(2,1)} fusion(bf16[2,256,2048]{2,1,0:T(8,128)(2,1)S(1)} %copy-done, bf16[1024,2048,1]{1,0,2:T(8,128)(2,1)} %reshape.73, bf16[2,2048,256]{2,1,0:T(8,128)(2,1)} %param.10, f32[1024,2]{0,1:T(2,128)S(1)} %compare_convert_fusion), kind=kOutput, calls=%fused_computation | convolution fusion | flops 4300210176 | bytes 12591104 | tf_op jit(solution)/shard_map/ref,efd->rd/dot_general | solution.py:41
  138.4 172.9 %all-reduce.2.cloned.1.call-done = bf16[1024,2048]{1,0:T(8,128)(2,1)} async-done(((bf16[1024,2048]{1,0:T(8,128)(2,1)}), bf16[1024,2048]{1,0:T(8,128)(2,1)}) %all-reduce.2.cloned.1.call-update) | async-done | bytes 4194320 | tf_op jit(solution)/shard_map/psum | solution.py:42
  311.2 0.9 convert_convert_fusion
  312.1 0.1 reshape.70
  312.2 19.0 %all_to_all.16 = bf16[16,2,2048]{2,1,0:T(2,128)(2,1)S(1)} all-to-all(bf16[16,2,2048]{2,1,0:T(2,128)(2,1)S(1)} %reshape.70), channel_id=1, replica_groups=mesh['group'=16,'inner'=32] {'group'}, dimensions={0} | all-to-all | bytes 262144 | tf_op jit(solution)/shard_map/all_to_all | solution.py:45
  331.3 0.8 fusion
  (13 shorter events, 0.3 us)
Async XLA Ops:
  6.5 122.3 %copy-start = (bf16[2,256,2048]{2,1,0:T(8,128)(2,1)S(1)}, bf16[2,256,2048]{2,1,0:T(8,128)(2,1)}, u32[]{:S(2)}) copy-start(bf16[2,256,2048]{2,1,0:T(8,128)(2,1)} %param.11) | copy-start | bytes 6291460
  6.5 106.6 %all-gather.2.cloned.1.call-start = ((), (), s32[]{:S(2)}) async-start(), calls=%async_computation.3 | async-start | bytes 4325376 | tf_op jit(solution)/shard_map/all_gather | solution.py:31
  30.8 9.9 %all-to-all-start.1 = ((bf16[1,16,2]{2,0,1:T(2,128)(2,1)}), bf16[1,16,2]{2,0,1:T(2,128)(2,1)S(1)}, u32[]{:S(2)}, u32[]{:S(2)}) async-start(bf16[1,16,2]{2,0,1:T(2,128)(2,1)} %reshape.78), calls=%async_computation.1 | async-start | bytes 16384 | tf_op jit(solution)/shard_map/all_to_all | solution.py:28
  34.1 277.1 %all-reduce.2.cloned.1.call-start = ((), (), s32[]{:S(2)}) async-start(), calls=%async_computation.4 | async-start | bytes 8388608 | tf_op jit(solution)/shard_map/psum | solution.py:42
  138.3 192.9 %copy-start.1 = (f32[16]{0:T(128)S(1)}, f32[16]{0:T(128)}, u32[]{:S(2)}) copy-start(f32[16]{0:T(128)} %param.9) | copy-start | bytes 196
Sparse Core Ops, SparseCore 0:
  29.4 83.6 all-gather.1
  138.5 172.6 all-reduce.1
where the time goes:
time: 339 us
  waiting for transfers between devices  214 us (63%)
  blocking collectives  74.7 us (22%)
  local copies, waits for them, and re-layouts  17.9 us (5%)
  between operations  13.5 us (4%)
  matrix products  12.1 us (4%)
  starting transfers between devices  3.41 us (1%)
  other arithmetic  3.41 us (1%)
    psum x1, waiting for transfers between devices, body(): lax.psum(every_term.astype(jnp.bfloat16), 'inner').astype(jnp.float32)  173 us
    all_gather x1, blocking collectives, body(): lax.all_gather(arrived_tags, 'inner', axis=0, tiled=True)  37.2 us
    all_gather x1, waiting for transfers between devices, body(): lax.all_gather(arrived, 'inner', axis=0, tiled=True)  34.5 us
    all_to_all x1, blocking collectives, body(): lax.all_to_all(send_back, 'group', split_axis=0, concat_axis=0, tiled=True)  19 us
    all_to_all x1, blocking collectives, body(): lax.all_to_all(outgoing, 'group', split_axis=1, concat_axis=1, tiled=True)  18.5 us
    dot_general x1, matrix products, body(): jnp.einsum('ref,efd->rd', hidden, w_down, preferred_element_type=jnp.floa...  9.51 us
    all_gather x1, local copies, waits for them, and re-layouts, body(): lax.all_gather(arrived, 'inner', axis=0, tiled=True)  8.52 us
    reshape x1, local copies, waits for them, and re-layouts, body(): slots = gathered.reshape(inner_size * groups * capacity, model_width)  7.19 us
  transfers between devices with their start and end apart: 3, of which 3 were waited for; matrix products, arithmetic and copies ran while one was open for 1% of the time, Pallas kernels for 0%

commit v1 on v0

--- a/solution.py
+++ b/solution.py
@@ -2,6 +2,22 @@
 import jax.numpy as jnp
 from jax import lax
 from jax.sharding import PartitionSpec as P
+
+
+def swapped_with_each(x, axis, split, join):
+    ways, here = (lax.axis_size(axis), lax.axis_index(axis))
+    width = x.shape[split] // ways
+    lengths = list(x.shape)
+    lengths[split] = width
+    height = lengths[join]
+    lengths[join] = height * ways
+    full = jnp.zeros(lengths, x.dtype)
+    for mask in range(ways):
+        part = lax.dynamic_slice_in_dim(x, (here ^ mask) * width, width, axis=split)
+        if mask:
+            part = lax.ppermute(part, axis, [(d, d ^ mask) for d in range(ways)])
+        full = lax.dynamic_update_slice_in_dim(full, part, (here ^ mask) * height, axis=join)
+    return full
 
 
 def body(pair_rows, group_ids, local_ids, route_weight, w_up, w_down):
@@ -24,7 +40,7 @@
     tags = jnp.dot(placing, tag_rows, preferred_element_type=jnp.float32).astype(jnp.bfloat16)
     tags = tags.reshape(1, groups, capacity)
     arrived, arrived_tags = (
-        lax.all_to_all(outgoing, "group", split_axis=1, concat_axis=1, tiled=True),
+        swapped_with_each(outgoing, "group", 1, 1),
         lax.all_to_all(tags, "group", split_axis=1, concat_axis=1, tiled=True),
     )
     gathered, gathered_tags = (

time: 339 us -> 387 us (1.14)
  starting transfers between devices: 3.41 us -> 65.1 us
  blocking collectives: 74.7 us -> 56 us
    ppermute x0 -> x15, starting transfers between devices: none -> 60.6 us  [swapped_with_each(): part = lax.ppermute(part, axis, [(d, d ^ mask) for d in range(ways)])]
    all_to_all x1 -> x0, blocking collectives: 18.5 us -> none  [body(): lax.all_to_all(outgoing, 'group', split_axis=1, concat_axis=1, tiled=True)]
  transfers between devices with their start and end apart: 3 -> 18, of which waited for: 3 -> 3; matrix products, arithmetic and copies ran while one was open for 1% -> 1% of each run, Pallas kernels for 0% -> 0%
where the time goes in v1:
time: 387 us; the launch traced here: 386 us
  waiting for transfers between devices  215 us (56%)
  starting transfers between devices  65.1 us (17%)
  blocking collectives  56 us (14%)
  local copies, waits for them, and re-layouts  20.6 us (5%)
  between operations  14.1 us (4%)
  matrix products  11.5 us (3%)
    psum x1, waiting for transfers between devices, body(): lax.psum(every_term.astype(jnp.bfloat16), 'inner').astype(jnp.float32)  173 us
    ppermute x15, starting transfers between devices, swapped_with_each(): part = lax.ppermute(part, axis, [(d, d ^ mask) for d in range(ways)])  60.6 us
    all_gather x1, blocking collectives, body(): lax.all_gather(arrived_tags, 'inner', axis=0, tiled=True)  37.1 us
    all_gather x1, waiting for transfers between devices, body(): lax.all_gather(arrived, 'inner', axis=0, tiled=True)  35.3 us
    all_to_all x1, blocking collectives, body(): lax.all_to_all(send_back, 'group', split_axis=0, concat_axis=0, tiled=True)  19 us
    dot_general x1, matrix products, body(): jnp.einsum('ref,efd->rd', hidden, w_down, preferred_element_type=jnp.floa...  9.53 us
    all_gather x1, local copies, waits for them, and re-layouts, body(): lax.all_gather(arrived, 'inner', axis=0, tiled=True)  8.54 us
  transfers between devices with their start and end apart: 18, of which 3 were waited for; matrix products, arithmetic and copies ran while one was open for 1% of the time, Pallas kernels for 0%

profile of v1, /device:TPU:1, one launch (start us, length us, event | category | flops | bytes accessed | tf_op | source)
XLA Modules:
  0.0 385.9 jit_solution(6148536147516319707)
XLA Ops:
  10.4 8.8 %collective-permute-start = (bf16[1,1,2,2048]{3,1,2,0:T(2,128)(2,1)S(1)}, bf16[1,1,2,2048]{3,1,2,0:T(2,128)(2,1)S(1)}, u32[]{:S(2)}, u32[]{:S(2)}) collective-permute-start(bf16[1,1,2,2048]{3,1,2,0:T(2,128)(2,1)S(1)} %copy.49), channel_id=1, source_target_pairs={{0,32},{32,0},{64,96},{96,64},{128,160},{160,128},{192,224},{224,1... | collective-permute-start | bytes 24584 | tf_op jit(solution)/shard_map/ppermute | solution.py:18
  19.2 1.9 collective-permute-start.1
  21.1 3.5 collective-permute-start.2
  24.7 1.9 collective-permute-start.3
  26.6 4.6 %collective-permute-start.4 = (bf16[1,1,2,2048]{3,1,2,0:T(2,128)(2,1)S(1)}, bf16[1,1,2,2048]{3,1,2,0:T(2,128)(2,1)S(1)}, u32[]{:S(2)}, u32[]{:S(2)}) collective-permute-start(bf16[1,1,2,2048]{3,1,2,0:T(2,128)(2,1)S(1)} %copy.53), channel_id=1, source_target_pairs={{0,160},{32,128},{64,224},{96,192},{128,32},{160,0},{192,96},{224,... | collective-permute-start | bytes 24584 | tf_op jit(solution)/shard_map/ppermute | solution.py:18
  31.4 1.9 collective-permute-start.5
  33.4 5.3 %collective-permute-start.6 = (bf16[1,1,2,2048]{3,1,2,0:T(2,128)(2,1)S(1)}, bf16[1,1,2,2048]{3,1,2,0:T(2,128)(2,1)S(1)}, u32[]{:S(2)}, u32[]{:S(2)}) collective-permute-start(bf16[1,1,2,2048]{3,1,2,0:T(2,128)(2,1)S(1)} %copy.55), channel_id=1, source_target_pairs={{0,224},{32,192},{64,160},{96,128},{128,96},{160,64},{192,32},{224... | collective-permute-start | bytes 24584 | tf_op jit(solution)/shard_map/ppermute | solution.py:18
  38.7 2.1 collective-permute-start.7
  40.8 7.5 %collective-permute-start.8 = (bf16[1,1,2,2048]{3,1,2,0:T(2,128)(2,1)S(1)}, bf16[1,1,2,2048]{3,1,2,0:T(2,128)(2,1)S(1)}, u32[]{:S(2)}, u32[]{:S(2)}) collective-permute-start(bf16[1,1,2,2048]{3,1,2,0:T(2,128)(2,1)S(1)} %copy.57), channel_id=1, source_target_pairs={{0,288},{32,256},{64,352},{96,320},{128,416},{160,384},{192,480},{... | collective-permute-start | bytes 24584 | tf_op jit(solution)/shard_map/ppermute | solution.py:18
  48.3 1.9 collective-permute-start.9
  50.4 6.5 %collective-permute-start.10 = (bf16[1,1,2,2048]{3,1,2,0:T(2,128)(2,1)S(1)}, bf16[1,1,2,2048]{3,1,2,0:T(2,128)(2,1)S(1)}, u32[]{:S(2)}, u32[]{:S(2)}) collective-permute-start(bf16[1,1,2,2048]{3,1,2,0:T(2,128)(2,1)S(1)} %copy.59), channel_id=1, source_target_pairs={{0,352},{32,320},{64,288},{96,256},{128,480},{160,448},{192,416},{... | collective-permute-start | bytes 24584 | tf_op jit(solution)/shard_map/ppermute | solution.py:18
  56.9 1.9 collective-permute-start.11
  58.9 5.9 %collective-permute-start.12 = (bf16[1,1,2,2048]{3,1,2,0:T(2,128)(2,1)S(1)}, bf16[1,1,2,2048]{3,1,2,0:T(2,128)(2,1)S(1)}, u32[]{:S(2)}, u32[]{:S(2)}) collective-permute-start(bf16[1,1,2,2048]{3,1,2,0:T(2,128)(2,1)S(1)} %copy.61), channel_id=1, source_target_pairs={{0,416},{32,384},{64,480},{96,448},{128,288},{160,256},{192,352},{... | collective-permute-start | bytes 24584 | tf_op jit(solution)/shard_map/ppermute | solution.py:18
  64.7 1.9 collective-permute-start.13
  66.7 4.8 %collective-permute-start.14 = (bf16[1,1,2,2048]{3,1,2,0:T(2,128)(2,1)S(1)}, bf16[1,1,2,2048]{3,1,2,0:T(2,128)(2,1)S(1)}, u32[]{:S(2)}, u32[]{:S(2)}) collective-permute-start(bf16[1,1,2,2048]{3,1,2,0:T(2,128)(2,1)S(1)} %copy.63), channel_id=1, source_target_pairs={{0,480},{32,448},{64,416},{96,384},{128,352},{160,320},{192,288},{... | collective-permute-start | bytes 24584 | tf_op jit(solution)/shard_map/ppermute | solution.py:18
  75.5 4.5 %all-to-all-start = ((bf16[1,16,2]{2,0,1:T(2,128)(2,1)}), bf16[1,16,2]{2,0,1:T(2,128)(2,1)S(1)}, u32[]{:S(2)}, u32[]{:S(2)}) async-start(bf16[1,16,2]{2,0,1:T(2,128)(2,1)} %reshape.78), calls=%async_computation | async-start | bytes 16384 | tf_op jit(solution)/shard_map/all_to_all | solution.py:44
  80.0 6.9 %all-to-all-done = bf16[1,16,2]{2,0,1:T(2,128)(2,1)S(1)} async-done(((bf16[1,16,2]{2,0,1:T(2,128)(2,1)}), bf16[1,16,2]{2,0,1:T(2,128)(2,1)S(1)}, u32[]{:S(2)}, u32[]{:S(2)}) %all-to-all-start) | async-done | bytes 96 | tf_op jit(solution)/shard_map/all_to_all | solution.py:44
  87.0 37.1 %all_gather.7 = bf16[32,16,2]{1,2,0:T(2,128)(2,1)S(1)} all-gather(bf16[1,16,2]{1,2,0:T(2,128)(2,1)S(1)} %copy.45), channel_id=1, replica_groups=mesh['group'=16,'inner'=32] {'inner'}, dimensions={0}, use_global_device_ids=true | all-gather | bytes 2112 | tf_op jit(solution)/shard_map/all_gather | solution.py:48
  124.6 35.3 %all-gather.2.cloned.1.call-done = bf16[32,16,2,2048]{3,1,2,0:T(8,128)(2,1)} async-done(((bf16[1,16,2,2048]{3,1,2,0:T(8,128)(2,1)}), bf16[32,16,2,2048]{3,1,2,0:T(8,128)(2,1)}) %all-gather.2.cloned.1.call-update) | async-done | bytes 4194320 | tf_op jit(solution)/shard_map/all_gather | solution.py:47
  159.9 8.5 %copy.43 = bf16[32,16,2,2048]{3,2,1,0:T(2,128)(2,1)} copy(bf16[32,16,2,2048]{3,1,2,0:T(8,128)(2,1)} %all-gather.2.cloned.1.call-done) | data formatting | bytes 8388608 | tf_op jit(solution)/shard_map/all_gather | solution.py:47
  168.5 7.2 %reshape.73 = bf16[1024,2048,1]{1,0,2:T(8,128)(2,1)} reshape(bf16[32,16,2,2048]{3,2,1,0:T(2,128)(2,1)} %copy.43) | data formatting | bytes 8388608 | tf_op jit(solution)/shard_map/reshape | solution.py:50
  175.7 9.5 %bitcast_convert_fusion = bf16[1024,2048]{1,0:T(8,128)(2,1)} fusion(bf16[2,256,2048]{2,1,0:T(8,128)(2,1)S(1)} %copy-done, bf16[1024,2048,1]{1,0,2:T(8,128)(2,1)} %reshape.73, bf16[2,2048,256]{2,1,0:T(8,128)(2,1)} %param.10, f32[1024,2]{0,1:T(2,128)S(1)} %compare_convert_fusion), kind=kOutput, calls=%fused_computation | convolution fusion | flops 4300210176 | bytes 12591104 | tf_op jit(solution)/shard_map/ref,efd->rd/dot_general | solution.py:57
  185.2 173.0 %all-reduce.2.cloned.1.call-done = bf16[1024,2048]{1,0:T(8,128)(2,1)} async-done(((bf16[1024,2048]{1,0:T(8,128)(2,1)}), bf16[1024,2048]{1,0:T(8,128)(2,1)}) %all-reduce.2.cloned.1.call-update) | async-done | bytes 4194320 | tf_op jit(solution)/shard_map/psum | solution.py:58
  359.2 19.0 %all_to_all.10 = bf16[16,2,2048]{2,1,0:T(2,128)(2,1)S(1)} all-to-all(bf16[16,2,2048]{2,1,0:T(2,128)(2,1)S(1)} %reshape.70), channel_id=1, replica_groups=mesh['group'=16,'inner'=32] {'group'}, dimensions={0} | all-to-all | bytes 262144 | tf_op jit(solution)/shard_map/all_to_all | solution.py:61
  (79 shorter events, 10.4 us)
Async XLA Ops:
  6.5 169.1 %copy-start = (bf16[2,256,2048]{2,1,0:T(8,128)(2,1)S(1)}, bf16[2,256,2048]{2,1,0:T(8,128)(2,1)}, u32[]{:S(2)}) copy-start(bf16[2,256,2048]{2,1,0:T(8,128)(2,1)} %param.11) | copy-start | bytes 6291460
  6.5 68.1 %copy-start.3 = (s32[16,1]{0,1:T(1,128)S(1)}, s32[16,1]{0,1:T(1,128)}, u32[]{:S(2)}) copy-start(s32[16,1]{0,1:T(1,128)} %param.8) | copy-start | bytes 196
  6.5 153.4 %all-gather.2.cloned.1.call-start = ((), (), s32[]{:S(2)}) async-start(), calls=%async_computation.2 | async-start | bytes 4325376 | tf_op jit(solution)/shard_map/all_gather | solution.py:47
  10.4 21.1 %collective-permute-start = (bf16[1,1,2,2048]{3,1,2,0:T(2,128)(2,1)S(1)}, bf16[1,1,2,2048]{3,1,2,0:T(2,128)(2,1)S(1)}, u32[]{:S(2)}, u32[]{:S(2)}) collective-permute-start(bf16[1,1,2,2048]{3,1,2,0:T(2,128)(2,1)S(1)} %copy.49), channel_id=1, source_target_pairs={{0,32},{32,0},{64,96},{96,64},{128,160},{160,128},{192,224},{224,1... | collective-permute-start | bytes 24584 | tf_op jit(solution)/shard_map/ppermute | solution.py:18
  19.2 14.2 %collective-permute-start.1 = (bf16[1,1,2,2048]{3,1,2,0:T(2,128)(2,1)S(1)}, bf16[1,1,2,2048]{3,1,2,0:T(2,128)(2,1)S(1)}, u32[]{:S(2)}, u32[]{:S(2)}) collective-permute-start(bf16[1,1,2,2048]{3,1,2,0:T(2,128)(2,1)S(1)} %copy.50), channel_id=1, source_target_pairs={{0,64},{32,96},{64,0},{96,32},{128,192},{160,224},{192,128},{224,1... | collective-permute-start | bytes 24584 | tf_op jit(solution)/shard_map/ppermute | solution.py:18
  21.1 17.6 %collective-permute-start.2 = (bf16[1,1,2,2048]{3,1,2,0:T(2,128)(2,1)S(1)}, bf16[1,1,2,2048]{3,1,2,0:T(2,128)(2,1)S(1)}, u32[]{:S(2)}, u32[]{:S(2)}) collective-permute-start(bf16[1,1,2,2048]{3,1,2,0:T(2,128)(2,1)S(1)} %copy.51), channel_id=1, source_target_pairs={{0,96},{32,64},{64,32},{96,0},{128,224},{160,192},{192,160},{224,1... | collective-permute-start | bytes 24584 | tf_op jit(solution)/shard_map/ppermute | solution.py:18
  24.7 16.1 %collective-permute-start.3 = (bf16[1,1,2,2048]{3,1,2,0:T(2,128)(2,1)S(1)}, bf16[1,1,2,2048]{3,1,2,0:T(2,128)(2,1)S(1)}, u32[]{:S(2)}, u32[]{:S(2)}) collective-permute-start(bf16[1,1,2,2048]{3,1,2,0:T(2,128)(2,1)S(1)} %copy.52), channel_id=1, source_target_pairs={{0,128},{32,160},{64,192},{96,224},{128,0},{160,32},{192,64},{224,... | collective-permute-start | bytes 24584 | tf_op jit(solution)/shard_map/ppermute | solution.py:18
  26.6 21.7 %collective-permute-start.4 = (bf16[1,1,2,2048]{3,1,2,0:T(2,128)(2,1)S(1)}, bf16[1,1,2,2048]{3,1,2,0:T(2,128)(2,1)S(1)}, u32[]{:S(2)}, u32[]{:S(2)}) collective-permute-start(bf16[1,1,2,2048]{3,1,2,0:T(2,128)(2,1)S(1)} %copy.53), channel_id=1, source_target_pairs={{0,160},{32,128},{64,224},{96,192},{128,32},{160,0},{192,96},{224,... | collective-permute-start | bytes 24584 | tf_op jit(solution)/shard_map/ppermute | solution.py:18
  31.4 18.9 %collective-permute-start.5 = (bf16[1,1,2,2048]{3,1,2,0:T(2,128)(2,1)S(1)}, bf16[1,1,2,2048]{3,1,2,0:T(2,128)(2,1)S(1)}, u32[]{:S(2)}, u32[]{:S(2)}) collective-permute-start(bf16[1,1,2,2048]{3,1,2,0:T(2,128)(2,1)S(1)} %copy.54), channel_id=1, source_target_pairs={{0,192},{32,224},{64,128},{96,160},{128,64},{160,96},{192,0},{224,... | collective-permute-start | bytes 24584 | tf_op jit(solution)/shard_map/ppermute | solution.py:18
  33.4 23.6 %collective-permute-start.6 = (bf16[1,1,2,2048]{3,1,2,0:T(2,128)(2,1)S(1)}, bf16[1,1,2,2048]{3,1,2,0:T(2,128)(2,1)S(1)}, u32[]{:S(2)}, u32[]{:S(2)}) collective-permute-start(bf16[1,1,2,2048]{3,1,2,0:T(2,128)(2,1)S(1)} %copy.55), channel_id=1, source_target_pairs={{0,224},{32,192},{64,160},{96,128},{128,96},{160,64},{192,32},{224... | collective-permute-start | bytes 24584 | tf_op jit(solution)/shard_map/ppermute | solution.py:18
  38.7 20.2 %collective-permute-start.7 = (bf16[1,1,2,2048]{3,1,2,0:T(2,128)(2,1)S(1)}, bf16[1,1,2,2048]{3,1,2,0:T(2,128)(2,1)S(1)}, u32[]{:S(2)}, u32[]{:S(2)}) collective-permute-start(bf16[1,1,2,2048]{3,1,2,0:T(2,128)(2,1)S(1)} %copy.56), channel_id=1, source_target_pairs={{0,256},{32,288},{64,320},{96,352},{128,384},{160,416},{192,448},{... | collective-permute-start | bytes 24584 | tf_op jit(solution)/shard_map/ppermute | solution.py:18
  40.8 23.9 %collective-permute-start.8 = (bf16[1,1,2,2048]{3,1,2,0:T(2,128)(2,1)S(1)}, bf16[1,1,2,2048]{3,1,2,0:T(2,128)(2,1)S(1)}, u32[]{:S(2)}, u32[]{:S(2)}) collective-permute-start(bf16[1,1,2,2048]{3,1,2,0:T(2,128)(2,1)S(1)} %copy.57), channel_id=1, source_target_pairs={{0,288},{32,256},{64,352},{96,320},{128,416},{160,384},{192,480},{... | collective-permute-start | bytes 24584 | tf_op jit(solution)/shard_map/ppermute | solution.py:18
  48.3 18.4 %collective-permute-start.9 = (bf16[1,1,2,2048]{3,1,2,0:T(2,128)(2,1)S(1)}, bf16[1,1,2,2048]{3,1,2,0:T(2,128)(2,1)S(1)}, u32[]{:S(2)}, u32[]{:S(2)}) collective-permute-start(bf16[1,1,2,2048]{3,1,2,0:T(2,128)(2,1)S(1)} %copy.58), channel_id=1, source_target_pairs={{0,320},{32,352},{64,256},{96,288},{128,448},{160,480},{192,384},{... | collective-permute-start | bytes 24584 | tf_op jit(solution)/shard_map/ppermute | solution.py:18
  50.4 22.8 %collective-permute-start.10 = (bf16[1,1,2,2048]{3,1,2,0:T(2,128)(2,1)S(1)}, bf16[1,1,2,2048]{3,1,2,0:T(2,128)(2,1)S(1)}, u32[]{:S(2)}, u32[]{:S(2)}) collective-permute-start(bf16[1,1,2,2048]{3,1,2,0:T(2,128)(2,1)S(1)} %copy.59), channel_id=1, source_target_pairs={{0,352},{32,320},{64,288},{96,256},{128,480},{160,448},{192,416},{... | collective-permute-start | bytes 24584 | tf_op jit(solution)/shard_map/ppermute | solution.py:18
  56.9 16.4 %collective-permute-start.11 = (bf16[1,1,2,2048]{3,1,2,0:T(2,128)(2,1)S(1)}, bf16[1,1,2,2048]{3,1,2,0:T(2,128)(2,1)S(1)}, u32[]{:S(2)}, u32[]{:S(2)}) collective-permute-start(bf16[1,1,2,2048]{3,1,2,0:T(2,128)(2,1)S(1)} %copy.60), channel_id=1, source_target_pairs={{0,384},{32,416},{64,448},{96,480},{128,256},{160,288},{192,320},{... | collective-permute-start | bytes 24584 | tf_op jit(solution)/shard_map/ppermute | solution.py:18
  58.9 14.6 %collective-permute-start.12 = (bf16[1,1,2,2048]{3,1,2,0:T(2,128)(2,1)S(1)}, bf16[1,1,2,2048]{3,1,2,0:T(2,128)(2,1)S(1)}, u32[]{:S(2)}, u32[]{:S(2)}) collective-permute-start(bf16[1,1,2,2048]{3,1,2,0:T(2,128)(2,1)S(1)} %copy.61), channel_id=1, source_target_pairs={{0,416},{32,384},{64,480},{96,448},{128,288},{160,256},{192,352},{... | collective-permute-start | bytes 24584 | tf_op jit(solution)/shard_map/ppermute | solution.py:18
  64.7 8.9 %collective-permute-start.13 = (bf16[1,1,2,2048]{3,1,2,0:T(2,128)(2,1)S(1)}, bf16[1,1,2,2048]{3,1,2,0:T(2,128)(2,1)S(1)}, u32[]{:S(2)}, u32[]{:S(2)}) collective-permute-start(bf16[1,1,2,2048]{3,1,2,0:T(2,128)(2,1)S(1)} %copy.62), channel_id=1, source_target_pairs={{0,448},{32,480},{64,384},{96,416},{128,320},{160,352},{192,256},{... | collective-permute-start | bytes 24584 | tf_op jit(solution)/shard_map/ppermute | solution.py:18
  66.7 7.1 %collective-permute-start.14 = (bf16[1,1,2,2048]{3,1,2,0:T(2,128)(2,1)S(1)}, bf16[1,1,2,2048]{3,1,2,0:T(2,128)(2,1)S(1)}, u32[]{:S(2)}, u32[]{:S(2)}) collective-permute-start(bf16[1,1,2,2048]{3,1,2,0:T(2,128)(2,1)S(1)} %copy.63), channel_id=1, source_target_pairs={{0,480},{32,448},{64,416},{96,384},{128,352},{160,320},{192,288},{... | collective-permute-start | bytes 24584 | tf_op jit(solution)/shard_map/ppermute | solution.py:18
  74.0 0.7 copy-start.1
  75.5 11.4 %all-to-all-start = ((bf16[1,16,2]{2,0,1:T(2,128)(2,1)}), bf16[1,16,2]{2,0,1:T(2,128)(2,1)S(1)}, u32[]{:S(2)}, u32[]{:S(2)}) async-start(bf16[1,16,2]{2,0,1:T(2,128)(2,1)} %reshape.78), calls=%async_computation | async-start | bytes 16384 | tf_op jit(solution)/shard_map/all_to_all | solution.py:44
  80.0 278.2 %all-reduce.2.cloned.1.call-start = ((), (), s32[]{:S(2)}) async-start(), calls=%async_computation.3 | async-start | bytes 8388608 | tf_op jit(solution)/shard_map/psum | solution.py:58
  185.2 193.0 %copy-start.2 = (f32[16]{0:T(128)S(1)}, f32[16]{0:T(128)}, u32[]{:S(2)}) copy-start(f32[16]{0:T(128)} %param.9) | copy-start | bytes 196
Sparse Core Ops, SparseCore 0:
  74.8 85.1 all-gather.1
  185.3 172.7 all-reduce.1
